TPU v7x, 32 devices: a whole 2x2x4 slice. The times are simulated.
32 devices in a mesh: band: 4 (over x, core), fld: 8 (over z, y).
Axes of the slice: x: 2, y: 2, z: 4, core: 2. Of those that a mesh axis runs over, the one named last changes fastest.
Arguments:
- spectra: float32 [480, 32, 961], P('fld'), may hold values from -0.006 to 0.006
- pair_slot: int32 [480], replicated, may hold values from 0 to 479, each once
- land_column: int32 [32, 1920], P(('band', 'fld')), may hold values from 0 to 2047, as said below
- owner_map: int32 [32, 1920], P(('band', 'fld')), may hold values from 0 to 7, as said below
- owner_slot: int32 [32, 640], P(('band', 'fld')), may hold values from 0 to 1919, as said below
- state_start: float32 [16, 32, 1920], P(None, ('band', 'fld')), may hold values from -6 to 6
- targets: float32 [16, 32, 1920], P(None, ('band', 'fld')), may hold values from -6 to 6
- amplitudes: float32 [16], replicated, may hold values from -3 to 3
- weight_in: float32 [256, 33], replicated, may hold values from -1 to 1
- weight_out: float32 [16, 256], replicated, may hold values from -0.375 to 0.375
Outputs:
- final_state: float32 [16, 20480], P(None, ('band', 'fld'))
- param_grad: float32 [16, 20480], P(None, ('band', 'fld'))
- amplitude_grad: float32 [16], replicated
Inputs may be any that keep to these rules, and one draw needn't show every extreme that they name: `land_column`: within each row the 1920 entries are distinct. owner_map[r, j] = (owner_map[r, 0] + j) mod 8, so that owner_map[r, j] * 240 + j // 8 are distinct within a row. A row has from 1 to 1920 land cells, at its first columns; the counts of a band sum to 5120, one row of every band has 1920, and owner_map[r, 0] is a band's offset plus the land cells of the band's earlier rows, modulo 8. `owner_slot`: the entries of one device are distinct and each names a land cell of its band that owner_map sends to it; every device takes exactly 640 cells, and one row of every band sends 240 cells to every device of the band.
All inputs are finite; a program needn't handle non-finite values.
Results may differ from a plain program's by a relative error of at most 0.0003.
Values sent between devices are 32-bit elements; how exact they have to be, the bound alone decides.
No kernel may reach another device: no remote copies, remote signals or barrier semaphores. Data moves between devices by JAX's collectives and lax.ppermute only.
A program may use at most 64 MiB of HBM per device.

v0:
```python
import functools
import math

import jax
import jax.numpy as jnp
from jax import lax
from jax.experimental import pallas as pl
from jax.experimental.pallas import tpu as pltpu
from jax.sharding import PartitionSpec as P

FIELDS = 16
STATE = 16
UNITS = 256
WAVES = 960
LONS = 2048
LATS = 1024
STEPS = 4
ROW_MEAN = 640
COEFS = 961
ROW_MAX = 1920
PAIRS = 480
TIME_STEP = 0.25

LANES = 128
HALF = LANES // 2
COUNT_LANE = HALF - 1
COEF_PAD = 1024
LON_OUTER = LONS // LANES
WAVE_INNER = 16
VMEM_LIMIT = 60 * 1024 * 1024

f32 = jnp.float32
bf16 = jnp.bfloat16


def iota(shape, dim):
    return lax.broadcasted_iota(jnp.int32, shape, dim)


def sincos_turns(turns):
    part = turns - jnp.round(turns)
    quarter = jnp.round(4.0 * part)
    x = (part - 0.25 * quarter) * (2.0 * math.pi)
    y = x * x
    sine = x * (1.0 + y * (-1.0 / 6 + y * (1.0 / 120 + y * (-1.0 / 5040 + y * (1.0 / 362880)))))
    cosine = 1.0 + y * (-0.5 + y * (1.0 / 24 + y * (-1.0 / 720 + y * (1.0 / 40320))))
    swap = jnp.abs(quarter) == 1.0
    low_sine = jnp.where(swap, cosine, sine)
    low_cosine = jnp.where(swap, sine, cosine)
    sine_flip = (quarter == -1.0) | (jnp.abs(quarter) == 2.0)
    cosine_flip = (quarter == 1.0) | (jnp.abs(quarter) == 2.0)
    return jnp.where(sine_flip, -low_sine, low_sine), jnp.where(cosine_flip, -low_cosine, low_cosine)


def halves(x):
    high = x.astype(bf16)
    return high, (x - high.astype(f32)).astype(bf16)


def dot(a, b):
    return jnp.dot(a, b, preferred_element_type=f32)


def dot_last(a, b):
    return lax.dot_general(a, b, (((1,), (1,)), ((), ())), preferred_element_type=f32)


def pick(pieces, piece_at, lane_at, rows):
    count, load = pieces
    lane_full = jnp.broadcast_to(lane_at, (rows, LANES))
    total = None
    for i in range(count):
        got = jnp.take_along_axis(load(i), lane_full, axis=1)
        total = got if total is None else jnp.where(piece_at == i, got, total)
    return total


def fourier_kernel(nb, pc, cap, gc, pairs_ref, slot_ref, spec_ref, out_ref, tab, ab, thr, lhs):
    step = pl.program_id(0)
    lane = iota((nb, LANES), 1)

    @pl.when(step == 0)
    def _():
        band = lax.axis_index("band")
        first = lax.axis_index("fld") * pc
        odd = (2 * (band * nb + iota((nb, LANES), 0)) + 1).astype(f32) * (1.0 / (4 * LATS))
        for t in range(COEF_PAD // LANES):
            column = (lane + t * LANES).astype(f32)
            for part in range(2):
                sine, cosine = sincos_turns((column - part) * odd)
                high, low = halves(jnp.concatenate([cosine, sine], axis=0))
                for copy in range(2):
                    at = pl.ds(copy * COEF_PAD + t * LANES, LANES)
                    tab[part, 0 : 2 * nb, at] = high
                    tab[part, 2 * nb : 4 * nb, at] = low
        thr[...] = jnp.zeros_like(thr)
        row = jnp.zeros((nb, LANES), f32)
        for s in range(pc):
            pair = pairs_ref[first + s]
            row = jnp.where(lane % HALF == s, pair.astype(f32), row)
            thr[s : s + 1, :] = jnp.full((1, LANES), WAVES - pair, jnp.int32)
        sine, cosine = sincos_turns(row * odd)
        is_odd = row - 2.0 * jnp.floor(row * 0.5) == 1.0
        ab[0] = jnp.where(is_odd, sine, cosine)
        ab[1] = jnp.where(is_odd, cosine, -sine)
        ab[2] = jnp.where(is_odd, 1.0, 0.0)
        lhs[...] = jnp.zeros_like(lhs)

    for t in range(COEF_PAD // LANES):
        width = min(LANES, COEFS - t * LANES)
        first_part = (iota((pc, LANES), 1) + t * LANES < thr[:pc, :])[:, :width]
        for g in range(gc):
            x = spec_ref[:, g, pl.ds(t * LANES, width)]
            high = x.astype(bf16).astype(f32)
            low = x - high
            for k, value in enumerate((high, low)):
                at = pl.ds(k * COEF_PAD + t * LANES, width)
                lhs[0, g * HALF : g * HALF + pc, at] = jnp.where(first_part, value, 0.0).astype(bf16)
                lhs[1, g * HALF : g * HALF + pc, at] = jnp.where(first_part, 0.0, value).astype(bf16)
    sums = []
    for part in range(2):
        both = dot_last(tab[part], lhs[part])
        sums.append(both[: 2 * nb] + both[2 * nb :])
    alpha, beta, is_odd = ab[0], ab[1], ab[2] > 0.0
    low_half = lane < HALF
    for i in range(gc // 2):
        at = slice(i * LANES, (i + 1) * LANES)
        wave0 = alpha * sums[0][:nb, at] + beta * sums[0][nb:, at]
        wave1 = jnp.where(is_odd, sums[1][:nb, at], sums[1][nb:, at])
        out_ref[:, 2 * i, :] = jnp.where(low_half, wave0, pltpu.roll(wave1, HALF, 1))
        out_ref[:, 2 * i + 1, :] = jnp.where(low_half, pltpu.roll(wave0, HALF, 1), wave1)

    @pl.when(step == 0)
    def _():
        slot = jnp.broadcast_to(slot_ref[...], (nb, slot_ref.shape[1]))
        below = iota((nb, slot_ref.shape[1]), 0) * cap
        count = jnp.sum(jnp.where((slot >= below) & (slot < below + cap), 1.0, 0.0), axis=1, keepdims=True)
        out_ref[:, 0, :] = jnp.where(lane == COUNT_LANE, count, out_ref[:, 0, :])


def fourier_call(nb, pc, cap, pair_slot, owner_slot, spectra):
    gc = 8
    return pl.pallas_call(
        functools.partial(fourier_kernel, nb, pc, cap, gc),
        grid=(2 * FIELDS // gc,),
        in_specs=[
            pl.BlockSpec(memory_space=pltpu.SMEM),
            pl.BlockSpec(owner_slot.shape, lambda i: (0, 0)),
            pl.BlockSpec((pc, gc, COEFS), lambda i: (0, i, 0)),
        ],
        out_specs=pl.BlockSpec((nb, gc, LANES), lambda i: (0, i, 0)),
        out_shape=jax.ShapeDtypeStruct((nb, 2 * FIELDS, LANES), f32),
        scratch_shapes=[
            pltpu.VMEM((2, 4 * nb, 2 * COEF_PAD), bf16),
            pltpu.VMEM((3, nb, LANES), f32),
            pltpu.VMEM((HALF, LANES), jnp.int32),
            pltpu.VMEM((2, gc * HALF, 2 * COEF_PAD), bf16),
        ],
        compiler_params=pltpu.CompilerParams(vmem_limit_bytes=VMEM_LIMIT),
        name="fourier",
    )(pair_slot, owner_slot, spectra)


def prepare_kernel(nb, pc, cp, pairs_ref, land_ref, state_ref, target_ref, amp_ref, win_ref, wout_ref,
                   cells_ref, place_ref, inverse_ref, dft_ref, turn_ref, amps_ref,
                   wx_ref, wo_ref, wt_ref, wb_ref):
    lane = iota((1, LANES), 1)
    source_pieces = ROW_MAX // LANES
    row = lax.axis_index("band") * nb + lax.axis_index("fld")
    odd = (2 * row + 1).astype(f32) * (0.5 / (2 * LATS))
    sin_colat = sincos_turns(jnp.full((8, LANES), 1.0, f32) * odd)[0]
    joined = 2 * STATE
    for m in range(nb):
        for q in range(cp // LANES):
            source = nb * (q * LANES + lane) + m
            first = nb * q
            count = min(nb, source_pieces - first)
            at = pl.ds(m * cp + q * LANES, LANES)
            piece_at, lane_at = source // LANES - first, source % LANES

            def load(ref, i):
                return ref[:, 0, pl.ds((first + i) * LANES, LANES)]

            for k, ref in enumerate((state_ref, target_ref)):
                cells_ref[k * STATE : (k + 1) * STATE, at] = pick(
                    (count, functools.partial(load, ref)), piece_at, lane_at, STATE
                )

            def load_land(i):
                return jnp.broadcast_to(land_ref[:, pl.ds((first + i) * LANES, LANES)], (8, LANES))

            column = pick((count, load_land), piece_at, lane_at, 8)
            hour = iota((8, LANES), 0).astype(f32)
            turns = column.astype(f32) * (1.0 / LONS) + hour * (1.0 / 24.0)
            forcing = jnp.maximum(sincos_turns(turns)[1], 0.0) * sin_colat
            place_ref[:, at] = jnp.where(iota((8, LANES), 0) < STEPS, forcing, column.astype(f32))
    for q in range(WAVE_INNER // 2):
        natural = lane + q * LANES
        wave = (natural % HALF) * WAVE_INNER + natural // HALF
        pair = jnp.minimum(wave, WAVES - 1 - wave)
        total = jnp.zeros((8, LANES), jnp.int32)
        rows = iota((8, LANES), 0)
        for i in range(PAIRS // 8):
            here = i * 8 + rows
            arrives = here + ((here.astype(f32) + 0.5) * (1.0 / pc)).astype(jnp.int32) * (LANES - pc)
            total = total + jnp.where(pairs_ref[i * 8 : i * 8 + 8, :] == pair, arrives, 0)
        found = jnp.sum(total.astype(f32), axis=0, keepdims=True).astype(jnp.int32)
        inverse_ref[:, pl.ds(q * LANES, LANES)] = jnp.broadcast_to(
            found + jnp.where(wave >= PAIRS, HALF, 0), (8, LANES)
        )
    a = iota((HALF, LANES), 0)
    sine, cosine = sincos_turns((a * iota((HALF, LANES), 1)).astype(f32) * (1.0 / LANES))
    table = jnp.concatenate(
        [jnp.concatenate([cosine, sine], axis=1), jnp.concatenate([-sine, cosine], axis=1)], axis=0
    )
    high, low = halves(table)
    dft_ref[0:LANES, :] = high
    dft_ref[LANES : 2 * LANES, :] = high
    dft_ref[2 * LANES : 3 * LANES, :] = low
    b = iota((WAVE_INNER, LANES), 0)
    sine, cosine = sincos_turns((b * iota((WAVE_INNER, LANES), 1)).astype(f32) * (1.0 / LONS))
    turn_ref[0:WAVE_INNER, :] = cosine
    turn_ref[WAVE_INNER : 2 * WAVE_INNER, :] = sine
    amp = jnp.broadcast_to(amp_ref[...], (FIELDS, FIELDS))
    diagonal = iota((FIELDS, FIELDS), 0) == iota((FIELDS, FIELDS), 1)
    amps_ref[...] = jnp.broadcast_to(
        jnp.sum(jnp.where(diagonal, amp, 0.0), axis=1, keepdims=True), (FIELDS, LANES)
    )
    win = win_ref[...]
    wout = wout_ref[...]
    high, low = halves(win)
    s, p = slice(0, STATE), slice(STATE, joined)
    tail = jnp.where(iota((UNITS, STATE), 1) == 0, high[:, joined:].astype(f32), 0.0)
    tail = jnp.where(iota((UNITS, STATE), 1) == 1, low[:, joined:].astype(f32), tail)
    tail = jnp.where(iota((UNITS, STATE), 1) == 2, high[:, joined:].astype(f32), tail)
    hf, lf = high.astype(f32), low.astype(f32)
    wx_ref[...] = jnp.concatenate(
        [hf[:, s], lf[:, s], hf[:, s], hf[:, p], lf[:, p], hf[:, p], tail], axis=1
    ).astype(bf16)
    turned = jnp.transpose(win)[:joined]
    high, low = halves(turned)
    wt_ref[0:joined, :] = high
    wt_ref[joined : 2 * joined, :] = low
    high, low = halves(wout)
    wo_ref[0:STATE, :] = high
    wo_ref[STATE : 2 * STATE, :] = low
    turned = jnp.transpose(wout)
    high, low = halves(turned)
    hf, lf = high.astype(f32), low.astype(f32)
    wb_ref[...] = jnp.concatenate([hf, lf, hf], axis=1).astype(bf16)


def prepare_call(nb, pc, cp, *arrays):
    length = nb * cp
    shapes = [
        ((2 * STATE, length), f32),
        ((8, length), f32),
        ((8, WAVE_INNER * HALF), jnp.int32),
        ((3 * LANES, 2 * LANES), bf16),
        ((2 * WAVE_INNER, LANES), f32),
        ((FIELDS, LANES), f32),
        ((UNITS, 6 * STATE + 16), bf16),
        ((2 * STATE, UNITS), bf16),
        ((4 * STATE, UNITS), bf16),
        ((UNITS, 3 * STATE), bf16),
    ]
    return pl.pallas_call(
        functools.partial(prepare_kernel, nb, pc, cp),
        out_shape=[jax.ShapeDtypeStruct(*s) for s in shapes],
        compiler_params=pltpu.CompilerParams(vmem_limit_bytes=VMEM_LIMIT),
        name="prepare",
    )(*arrays)


def advance_kernel(nb, cp, ndev, lc, owner_ref, arrived_ref, inverse_ref, dft_ref, turn_ref, amps_ref, cells_ref,
                   place_ref, wx_ref, wo_ref, wt_ref, wb_ref, out_ref, copies_ref,
                   grid_ref, pattern_ref, param_ref, force_ref, state_ref, slope_ref, adj_ref, grad_ref):
    length = nb * cp
    lane = iota((1, LANES), 1)
    rows = iota((FIELDS, LANES), 1)
    low_half = rows < HALF
    blocks = []
    for q in range(WAVE_INNER // 2):
        natural = lane + q * LANES
        wave = (natural % HALF) * WAVE_INNER + natural // HALF
        at = inverse_ref[0:1, pl.ds(q * LANES, LANES)]
        x = pick((nb, lambda i: arrived_ref[i]), at // LANES, at % LANES, 2 * FIELDS)
        x = jnp.where(wave < WAVES, x * jnp.where(wave == 0, 1.0, 2.0), 0.0)
        real, imag = x[:FIELDS], x[FIELDS:]
        blocks.append(jnp.where(low_half, real, pltpu.roll(imag, HALF, 1)))
        blocks.append(jnp.where(low_half, pltpu.roll(real, HALF, 1), imag))
    coeffs = jnp.concatenate(blocks, axis=0)
    high, low = halves(coeffs)
    partial = dot(high, dft_ref[0:LANES]) + dot(low, dft_ref[0:LANES]) + dot(high, dft_ref[2 * LANES : 3 * LANES])
    reals, imags = [], []
    for b in range(WAVE_INNER):
        y_real = partial[b * FIELDS : (b + 1) * FIELDS, :LANES]
        y_imag = partial[b * FIELDS : (b + 1) * FIELDS, LANES:]
        cosine, sine = turn_ref[b : b + 1, :], turn_ref[WAVE_INNER + b : WAVE_INNER + b + 1, :]
        reals.append(y_real * cosine - y_imag * sine)
        imags.append(y_real * sine + y_imag * cosine)
    half = WAVE_INNER // 2
    sums = [reals[b] + reals[WAVE_INNER - b] for b in range(1, half)]
    gaps = [imags[b] - imags[WAVE_INNER - b] for b in range(1, half)]
    for c in range(half + 1):
        even = reals[0] + reals[half] if c % 2 == 0 else reals[0] - reals[half]
        odd = None
        for b in range(1, half):
            turn = 2.0 * math.pi * (b * c % WAVE_INNER) / WAVE_INNER
            even = even + math.cos(turn) * sums[b - 1]
            term = math.sin(turn) * gaps[b - 1]
            odd = term if odd is None else odd + term
        grid_ref[c] = even - odd
        if 0 < c < half:
            grid_ref[WAVE_INNER - c] = even + odd
    amps = amps_ref[...]
    for q in range(length // LANES):
        at = pl.ds(q * LANES, LANES)
        column = place_ref[STEPS : STEPS + 1, at].astype(jnp.int32)
        found = pick((LON_OUTER, lambda i: grid_ref[i]), column // LANES, column % LANES, FIELDS)
        pattern_ref[:, at] = found
        high, low = halves(amps * found)
        param_ref[0:FIELDS, at] = high
        param_ref[FIELDS : 2 * FIELDS, at] = high
        param_ref[2 * FIELDS : 3 * FIELDS, at] = low
        row16 = iota((16, LANES), 0)
        for t in range(STEPS):
            force = place_ref[t : t + 1, at]
            force_high = force.astype(bf16).astype(f32)
            packed = jnp.where(row16 < 2, force_high, jnp.where(row16 == 2, force - force_high, 0.0))
            force_ref[t, :, at] = packed.astype(bf16)
    state_ref[...] = cells_ref[0:STATE, :]
    spans = [pl.ds(i * lc, lc) for i in range(length // lc)]
    wx, wo, wt, wb = wx_ref[...], wo_ref[...], wt_ref[...], wb_ref[...]
    for t in range(STEPS):
        for at in spans:
            state = state_ref[:, at]
            high, low = halves(state)
            joined = jnp.concatenate([high, high, low, param_ref[:, at], force_ref[t, :, at]], axis=0)
            hidden = jnp.tanh(dot(wx, joined))
            slope_ref[t, :, at] = 1.0 - hidden * hidden
            high, low = halves(hidden)
            moved = dot(wo, high)
            moved = moved[:STATE] + moved[STATE:] + dot(wo[:STATE], low)
            state_ref[:, at] = state + TIME_STEP * moved
    for t in reversed(range(STEPS)):
        for at in spans:
            if t == STEPS - 1:
                adjoint = state_ref[:, at] - cells_ref[STATE : 2 * STATE, at]
            else:
                adjoint = adj_ref[:, at]
            high, low = halves(TIME_STEP * adjoint)
            through = dot(wb, jnp.concatenate([high, high, low], axis=0)) * slope_ref[t, :, at]
            high, low = halves(through)
            both = dot(wt, high)
            both = both[: 2 * STATE] + both[2 * STATE :] + dot(wt[: 2 * STATE], low)
            adj_ref[:, at] = adjoint + both[:STATE]
            gained = both[STATE:]
            grad_ref[:, at] = gained if t == STEPS - 1 else grad_ref[:, at] + gained
    first_owner = owner_ref[0, 0]
    total = jnp.zeros((FIELDS, cp), f32)
    place = iota((FIELDS, cp), 1).astype(f32)
    for m in range(nb):
        owner = (first_owner + m) % nb
        at = pl.ds(m * cp, cp)
        grad = grad_ref[:, at]
        out_ref[owner, 0:STATE, :] = state_ref[:, at]
        out_ref[owner, STATE : 2 * STATE, :] = grad
        count = arrived_ref[owner, 0:1, COUNT_LANE : COUNT_LANE + 1]
        total = total + jnp.where(place < count, grad * pattern_ref[:, at], 0.0)
    summed = jnp.sum(total, axis=1, keepdims=True)
    diagonal = iota((FIELDS, FIELDS), 0) == iota((FIELDS, FIELDS), 1)
    along = jnp.sum(jnp.where(diagonal, summed, 0.0), axis=0, keepdims=True)
    copies_ref[...] = jnp.broadcast_to(along, (ndev, FIELDS))


def advance_call(nb, cp, ndev, owner_map, arrived, prepared):
    cells, place, inverse, dft, turn, amps, wx, wo, wt, wb = prepared
    length = nb * cp
    lc = 512
    vmem = pl.BlockSpec(memory_space=pltpu.VMEM)
    return pl.pallas_call(
        functools.partial(advance_kernel, nb, cp, ndev, lc),
        in_specs=[pl.BlockSpec(memory_space=pltpu.SMEM)] + [vmem] * 11,
        out_shape=[
            jax.ShapeDtypeStruct((nb, 2 * STATE, cp), f32),
            jax.ShapeDtypeStruct((ndev, FIELDS), f32),
        ],
        scratch_shapes=[
            pltpu.VMEM((LON_OUTER, FIELDS, LANES), f32),
            pltpu.VMEM((FIELDS, length), f32),
            pltpu.VMEM((3 * FIELDS, length), bf16),
            pltpu.VMEM((STEPS, 16, length), bf16),
            pltpu.VMEM((STATE, length), f32),
            pltpu.VMEM((STEPS, UNITS, length), f32),
            pltpu.VMEM((STATE, length), f32),
            pltpu.VMEM((FIELDS, length), f32),
        ],
        compiler_params=pltpu.CompilerParams(vmem_limit_bytes=VMEM_LIMIT),
        name="advance",
    )(owner_map[:, :LANES], arrived, inverse, dft, turn, amps, cells, place, wx, wo, wt, wb)


def owned_kernel(nb, cap, cp, scale, slot_ref, received_ref, parts_ref, final_ref, grad_ref, amp_ref):
    per_row = cp // LANES
    for q in range(slot_ref.shape[1] // LANES):
        at = pl.ds(q * LANES, LANES)
        slot = slot_ref[:, at]
        row = ((slot.astype(f32) + 0.5) * (1.0 / cap)).astype(jnp.int32)
        place = slot - row * cap
        piece = row * per_row + place // LANES

        def load(i):
            return received_ref[i // per_row, :, pl.ds(i % per_row * LANES, LANES)]

        found = pick((nb * per_row, load), piece, place % LANES, 2 * STATE)
        final_ref[:, at] = found[:STATE]
        grad_ref[:, at] = found[STATE:]
    amp_ref[...] = jnp.sum(parts_ref[...], axis=0, keepdims=True) * scale


def owned_call(nb, cap, cp, scale, owner_slot, received, parts):
    mean = owner_slot.shape[1]
    return pl.pallas_call(
        functools.partial(owned_kernel, nb, cap, cp, scale),
        out_shape=[
            jax.ShapeDtypeStruct((STATE, mean), f32),
            jax.ShapeDtypeStruct((FIELDS, mean), f32),
            jax.ShapeDtypeStruct((1, FIELDS), f32),
        ],
        compiler_params=pltpu.CompilerParams(vmem_limit_bytes=VMEM_LIMIT),
        name="owned",
    )(owner_slot, received, parts)


def body(
    spectra,
    pair_slot,
    land_column,
    owner_map,
    owner_slot,
    state_start,
    targets,
    amplitudes,
    weight_in,
    weight_out,
):
    nb = lax.axis_size("fld")
    ndev = lax.axis_size("band") * nb
    pc = spectra.shape[0]
    cap = ROW_MAX // nb
    cp = -(-cap // LANES) * LANES
    coeffs = fourier_call(nb, pc, cap, pair_slot, owner_slot, spectra)
    arrived = lax.all_to_all(coeffs, "fld", split_axis=0, concat_axis=0, tiled=True)
    prepared = prepare_call(
        nb, pc, cp, jnp.broadcast_to(pair_slot[:, None], (PAIRS, LANES)), land_column, state_start, targets,
        amplitudes[None, :], weight_in, weight_out,
    )
    outbound, copies = advance_call(nb, cp, ndev, owner_map, arrived, prepared)
    received = lax.all_to_all(outbound, "fld", split_axis=0, concat_axis=0, tiled=True)
    parts = lax.all_to_all(copies, ("band", "fld"), split_axis=0, concat_axis=0, tiled=True)
    scale = 1.0 / math.sqrt(ndev * ROW_MEAN)
    final_state, param_grad, amplitude_grad = owned_call(nb, cap, cp, scale, owner_slot, received, parts)
    return (final_state, param_grad, amplitude_grad[0])


def solution(mesh):
    return jax.shard_map(
        body,
        mesh=mesh,
        in_specs=(
            P("fld", None, None),
            P(),
            P(("band", "fld"), None),
            P(("band", "fld"), None),
            P(("band", "fld"), None),
            P(None, ("band", "fld"), None),
            P(None, ("band", "fld"), None),
            P(),
            P(),
            P(),
        ),
        out_specs=(P(None, ("band", "fld")), P(None, ("band", "fld")), P()),
        check_vma=False,
    )
```

profile of v0, /device:TPU:0, one launch (start us, length us, event | category | flops | bytes accessed | tf_op | source)
XLA Modules:
  0.0 77.1 jit_solution(11726770115947178121)
XLA Ops:
  0.6 0.0 copy-start.2
  0.6 0.0 copy-start.1
  0.7 24.2 %fourier.1 = f32[8,32,128]{2,1,0:T(8,128)} custom-call(s32[480]{0:T(512)} %pairs_ref.1, s32[1,640]{1,0:T(1,128)} %slot_ref.3, f32[60,32,961]{2,1,0:T(8,128)} %spec_ref.1), custom_call_target="tpu_custom_call" | custom-call | tf_op jit(solution)/shard_map/fourier/pallas_call | solution.py:143
  24.8 7.3 %all-to-all-start = ((f32[8,32,128]{2,1,0:T(8,128)}), f32[8,32,128]{2,1,0:T(8,128)S(1)}, u32[]{:S(2)}, u32[]{:S(2)}) async-start(f32[8,32,128]{2,1,0:T(8,128)} %fourier.1), calls=%async_computation | async-start | bytes 262144 | tf_op jit(solution)/shard_map/all_to_all | solution.py:454
  32.1 0.0 copy-done.1
  32.1 0.8 copy.14.win_ref
  32.9 1.2 %slice.3.owner_ref = s32[1,128]{1,0:T(1,128)} slice(s32[1,1920]{1,0:T(1,128)} %param.13), slice={[0:1], [0:128]} | slice | bytes 1024 | tf_op jit(solution)/shard_map/slice | solution.py:401
  34.1 0.0 copy-done.2
  34.1 0.8 %broadcast_in_dim.4.pairs_ref = s32[480,128]{1,0:T(8,128)} broadcast(s32[480]{0:T(512)S(1)} %copy-done.2), dimensions={0} | broadcast | bytes 247680 | tf_op jit(solution)/shard_map/broadcast_in_dim | solution.py:456
  34.9 3.4 %prepare.1 = (f32[32,2048]{1,0:T(8,128)}, f32[8,2048]{1,0:T(8,128)}, s32[8,1024]{1,0:T(8,128)}, bf16[384,256]{1,0:T(8,128)(2,1)}, f32[32,128]{1,0:T(8,128)}, /*i...) custom-call(s32[480,128]{1,0:T(8,128)} %broadcast_in_dim.4.pairs_ref, ...), custom_call_target="tpu_custom_call" | custom-call | tf_op jit(solution)/shard_map/prepare/pallas_call | solution.py:267
  38.3 1.2 %all-to-all-done.arrived_ref = f32[8,32,128]{2,1,0:T(8,128)S(1)} async-done(((f32[8,32,128]{2,1,0:T(8,128)}), f32[8,32,128]{2,1,0:T(8,128)S(1)}, u32[]{:S(2)}, u32[]{:S(2)}) %all-to-all-start) | async-done | bytes 131104 | tf_op jit(solution)/shard_map/all_to_all | solution.py:454
  39.5 0.0 copy-start
  39.5 0.6 copy-done
  40.1 9.8 %advance.1 = (f32[8,32,256]{2,1,0:T(8,128)}, f32[32,16]{1,0:T(8,128)}) custom-call(s32[1,128]{1,0:T(1,128)} %slice.3.owner_ref, f32[8,32,128]{2,1,0:T(8,128)} %copy-done, s32[8,1024]{1,0:T(8,128)} %get-tuple-element.18.inverse_ref, bf16[384,256]{1,0:T(8,128)(2,1)} %get-tuple-element.19.dft_ref, f32[32,128]{1,0:T(8,128)} %get-tuple-element.20.turn_ref, ...), custom_call_target="tpu_custom_call" | custom-call | tf_op jit(solution)/shard_map/advance/pallas_call | solution.py:382
  49.9 12.1 %all_to_all.21 = f32[32,1,16]{2,1,0:T(1,128)} all-to-all(f32[32,1,16]{2,1,0:T(1,128)} %bitcast.7), channel_id=1, replica_groups=mesh['band'=4,'fld'=8] {'band','fld'}, dimensions={0} | all-to-all | bytes 4096 | tf_op jit(solution)/shard_map/all_to_all | solution.py:461
  62.0 13.1 %all_to_all.22.received_ref = f32[8,32,256]{2,1,0:T(8,128)} all-to-all(f32[8,32,256]{2,1,0:T(8,128)} %get-tuple-element.28), channel_id=1, replica_groups=mesh['band'=4,'fld'=8] {'fld'}, dimensions={0} | all-to-all | bytes 524288 | tf_op jit(solution)/shard_map/all_to_all | solution.py:460
  75.0 2.0 %owned.1 = (f32[16,640]{1,0:T(8,128)}, f32[16,640]{1,0:T(8,128)}, f32[1,16]{1,0:T(1,128)}) custom-call(s32[1,640]{1,0:T(1,128)} %slot_ref.3, f32[8,32,256]{2,1,0:T(8,128)} %all_to_all.22.received_ref, f32[32,16]{1,0:T(8,128)} %bitcast.6), custom_call_target="tpu_custom_call" | custom-call | tf_op jit(solution)/shard_map/owned/pallas_call | solution.py:424
Async XLA Ops:
  0.6 33.4 %copy-start.2 = (s32[480]{0:T(512)S(1)}, s32[480]{0:T(512)}, u32[]{:S(2)}) copy-start(s32[480]{0:T(512)} %pairs_ref.1) | copy-start | bytes 5764
  0.6 31.5 %copy-start.1 = (f32[256,33]{0,1:T(8,128)S(1)}, f32[256,33]{0,1:T(8,128)}, u32[]{:S(2)}) copy-start(f32[256,33]{0,1:T(8,128)} %param.18) | copy-start | bytes 101380
  24.8 14.6 %all-to-all-start = ((f32[8,32,128]{2,1,0:T(8,128)}), f32[8,32,128]{2,1,0:T(8,128)S(1)}, u32[]{:S(2)}, u32[]{:S(2)}) async-start(f32[8,32,128]{2,1,0:T(8,128)} %fourier.1), calls=%async_computation | async-start | bytes 262144 | tf_op jit(solution)/shard_map/all_to_all | solution.py:454
  39.5 0.6 copy-start
where the time goes:
time: 77.5 us; the launch traced here: 77.1 us
  Pallas kernels  39.4 us (51%)
  blocking collectives  25.1 us (32%)
  starting transfers between devices  7.28 us (9%)
  local copies, waits for them, and re-layouts  3.41 us (4%)
  waiting for transfers between devices  1.18 us (2%)
    pallas_call x1, Pallas kernels, fourier_call(): pl.pallas_call(functools.partial(fourier_kernel, nb, pc, cap, gc), grid=(...  24.2 us
    all_to_all x1, blocking collectives, body(): lax.all_to_all(outbound, 'fld', split_axis=0, concat_axis=0, tiled=True)  13.1 us
    all_to_all x1, blocking collectives, body(): lax.all_to_all(copies, ('band', 'fld'), split_axis=0, concat_axis=0, tile...  12.1 us
    pallas_call x1, Pallas kernels, advance_call(): pl.pallas_call(functools.partial(advance_kernel, nb, cp, ndev, lc), in_sp...  9.79 us
    all_to_all x1, starting transfers between devices, body(): lax.all_to_all(coeffs, 'fld', split_axis=0, concat_axis=0, tiled=True)  7.28 us
    pallas_call x1, Pallas kernels, prepare_call(): pl.pallas_call(functools.partial(prepare_kernel, nb, pc, cp), out_shape=[...  3.4 us
    pallas_call x1, Pallas kernels, owned_call(): pl.pallas_call(functools.partial(owned_kernel, nb, cap, cp, scale), out_s...  2.02 us
  transfers between devices with their start and end apart: 1, of which 1 were waited for; matrix products, arithmetic and copies ran while one was open for 4% of the time, Pallas kernels for 4%

commit v1 on v0

--- a/solution.py
+++ b/solution.py
@@ -25,6 +25,9 @@
 HALF = LANES // 2
 COUNT_LANE = HALF - 1
 COEF_PAD = 1024
+COEF_TILES = COEF_PAD // LANES
+LAST = COEFS - (COEF_TILES - 1) * LANES
+EARLY = (WAVES - PAIRS + 1) // LANES
 LON_OUTER = LONS // LANES
 WAVE_INNER = 16
 VMEM_LIMIT = 60 * 1024 * 1024
@@ -75,86 +78,119 @@
     return total
 
 
-def fourier_kernel(nb, pc, cap, gc, pairs_ref, slot_ref, spec_ref, out_ref, tab, ab, thr, lhs):
-    step = pl.program_id(0)
+def fourier_kernel(nb, pc, cap, gc, pairs_ref, slot_ref, spec_ref, out_ref, buf, tab, thr, lhs, tail, sem):
     lane = iota((nb, LANES), 1)
-
-    @pl.when(step == 0)
-    def _():
-        band = lax.axis_index("band")
-        first = lax.axis_index("fld") * pc
-        odd = (2 * (band * nb + iota((nb, LANES), 0)) + 1).astype(f32) * (1.0 / (4 * LATS))
-        for t in range(COEF_PAD // LANES):
-            column = (lane + t * LANES).astype(f32)
-            for part in range(2):
-                sine, cosine = sincos_turns((column - part) * odd)
-                high, low = halves(jnp.concatenate([cosine, sine], axis=0))
-                for copy in range(2):
-                    at = pl.ds(copy * COEF_PAD + t * LANES, LANES)
-                    tab[part, 0 : 2 * nb, at] = high
-                    tab[part, 2 * nb : 4 * nb, at] = low
-        thr[...] = jnp.zeros_like(thr)
-        row = jnp.zeros((nb, LANES), f32)
-        for s in range(pc):
-            pair = pairs_ref[first + s]
-            row = jnp.where(lane % HALF == s, pair.astype(f32), row)
-            thr[s : s + 1, :] = jnp.full((1, LANES), WAVES - pair, jnp.int32)
-        sine, cosine = sincos_turns(row * odd)
-        is_odd = row - 2.0 * jnp.floor(row * 0.5) == 1.0
-        ab[0] = jnp.where(is_odd, sine, cosine)
-        ab[1] = jnp.where(is_odd, cosine, -sine)
-        ab[2] = jnp.where(is_odd, 1.0, 0.0)
-        lhs[...] = jnp.zeros_like(lhs)
-
-    for t in range(COEF_PAD // LANES):
-        width = min(LANES, COEFS - t * LANES)
-        first_part = (iota((pc, LANES), 1) + t * LANES < thr[:pc, :])[:, :width]
+    rows = pc * gc
+    groups = 2 * FIELDS // gc
+    copies = []
+    for k in range(groups):
+        at = pl.ds(k * gc, gc)
+        copies.append(pltpu.make_async_copy(spec_ref.at[:, at, :], buf.at[:, at, :], sem.at[k]))
+        copies[k].start()
+    band = lax.axis_index("band")
+    first = lax.axis_index("fld") * pc
+    odd = (2 * (band * nb + iota((nb, LANES), 0)) + 1).astype(f32) * (1.0 / (4 * LATS))
+    for t in range(COEF_TILES):
+        column = lane + t * LANES
+        if t == COEF_TILES - 1:
+            column = jnp.where(lane < LAST, column, lane + EARLY * LANES)
+        sine, cosine = sincos_turns(column.astype(f32) * odd)
+        high, low = halves(jnp.concatenate([cosine, sine], axis=0))
+        at = pl.ds(t * LANES, LANES)
+        tab[0 : 2 * nb, at] = high
+        tab[2 * nb : 4 * nb, at] = low
+    row = jnp.zeros((nb, LANES), f32)
+    for s in range(pc):
+        pair = pairs_ref[first + s]
+        row = jnp.where(lane % HALF == s, pair.astype(f32), row)
+        thr[s * gc : (s + 1) * gc, :] = jnp.full((gc, LANES), WAVES - pair, jnp.int32)
+    sine, cosine = sincos_turns(row * odd)
+    is_odd = row - 2.0 * jnp.floor(row * 0.5) == 1.0
+    alpha = jnp.where(is_odd, sine, cosine)
+    beta = jnp.where(is_odd, cosine, -sine)
+    sine, cosine = sincos_turns(odd)
+    gamma = jnp.where(is_odd, cosine, -sine)
+    delta = jnp.where(is_odd, sine, cosine)
+    pieces = -(-rows // LANES)
+    wide = iota((rows, LANES), 1)
+    for k in range(groups):
+        copies[k].wait()
+        base = k * rows
+        here = slice(base, base + rows)
+        early = None
+        for t in range(COEF_TILES):
+            at = pl.ds(t * LANES, LANES)
+            if t < COEF_TILES - 1:
+                x = buf[:, k * gc : (k + 1) * gc, at].reshape(rows, LANES)
+            else:
+                x = buf[:, k * gc : (k + 1) * gc, t * LANES : COEFS].reshape(rows, LAST)
+                x = jnp.concatenate([x, jnp.zeros((rows, LANES - LAST), f32)], axis=1)
+            high = x.astype(bf16)
+            whole = high.astype(f32)
+            rest = x - whole
+            lhs[0, here, at] = high
+            lhs[1, here, at] = rest.astype(bf16)
+            if t == EARLY:
+                early = whole, rest
+            if t > EARLY:
+                column = wide + t * LANES
+                if t == COEF_TILES - 1:
+                    column = jnp.where(wide < LAST, column, wide + EARLY * LANES)
+                    whole = jnp.where(wide < LAST, whole, early[0])
+                    rest = jnp.where(wide < LAST, rest, early[1])
+                second = column >= thr[...]
+                at = pl.ds((t - EARLY - 1) * LANES, LANES)
+                tail[0, here, at] = jnp.where(second, whole, 0.0).astype(bf16)
+                tail[1, here, at] = jnp.where(second, rest, 0.0).astype(bf16)
+        end = slice((EARLY + 1) * LANES, COEF_PAD)
+        everything = contract(lhs[0, here, :], tab[...]) + contract(lhs[1, here, :], tab[...])
+        shifted = contract(tail[0, here, :], tab[:, end]) + contract(tail[1, here, :], tab[:, end])
+        everything = everything[: 2 * nb] + everything[2 * nb :]
+        shifted = shifted[: 2 * nb] + shifted[2 * nb :]
+        pad = [(0, 0), (0, pieces * LANES - rows)]
+        first_part, shifted = jnp.pad(everything - shifted, pad), jnp.pad(shifted, pad)
         for g in range(gc):
-            x = spec_ref[:, g, pl.ds(t * LANES, width)]
-            high = x.astype(bf16).astype(f32)
-            low = x - high
-            for k, value in enumerate((high, low)):
-                at = pl.ds(k * COEF_PAD + t * LANES, width)
-                lhs[0, g * HALF : g * HALF + pc, at] = jnp.where(first_part, value, 0.0).astype(bf16)
-                lhs[1, g * HALF : g * HALF + pc, at] = jnp.where(first_part, 0.0, value).astype(bf16)
-    sums = []
-    for part in range(2):
-        both = dot_last(tab[part], lhs[part])
-        sums.append(both[: 2 * nb] + both[2 * nb :])
-    alpha, beta, is_odd = ab[0], ab[1], ab[2] > 0.0
-    low_half = lane < HALF
-    for i in range(gc // 2):
-        at = slice(i * LANES, (i + 1) * LANES)
-        wave0 = alpha * sums[0][:nb, at] + beta * sums[0][nb:, at]
-        wave1 = jnp.where(is_odd, sums[1][:nb, at], sums[1][nb:, at])
-        out_ref[:, 2 * i, :] = jnp.where(low_half, wave0, pltpu.roll(wave1, HALF, 1))
-        out_ref[:, 2 * i + 1, :] = jnp.where(low_half, pltpu.roll(wave0, HALF, 1), wave1)
-
-    @pl.when(step == 0)
-    def _():
-        slot = jnp.broadcast_to(slot_ref[...], (nb, slot_ref.shape[1]))
-        below = iota((nb, slot_ref.shape[1]), 0) * cap
-        count = jnp.sum(jnp.where((slot >= below) & (slot < below + cap), 1.0, 0.0), axis=1, keepdims=True)
-        out_ref[:, 0, :] = jnp.where(lane == COUNT_LANE, count, out_ref[:, 0, :])
+            source = (iota((1, LANES), 1) % HALF) * gc + g
+            piece_at, lane_at = source // LANES, source % LANES
+
+            def gather(values):
+                return pick((pieces, lambda i: values[:, i * LANES : (i + 1) * LANES]), piece_at, lane_at, nb)
+
+            wave0 = alpha * gather(first_part[:nb]) + beta * gather(first_part[nb:])
+            wave1 = gamma * gather(shifted[:nb]) + delta * gather(shifted[nb:])
+            value = jnp.where(lane < HALF, wave0, wave1)
+            value = jnp.where(lane % HALF < pc, value, 0.0)
+            if k == 0 and g == 0:
+                slot = jnp.broadcast_to(slot_ref[...], (nb, slot_ref.shape[1]))
+                below = iota((nb, slot_ref.shape[1]), 0) * cap
+                inside = (slot >= below) & (slot < below + cap)
+                count = jnp.sum(jnp.where(inside, 1.0, 0.0), axis=1, keepdims=True)
+                value = jnp.where(lane == COUNT_LANE, count, value)
+            out_ref[:, k * gc + g, :] = value
+
+
+def contract(values, table):
+    return jnp.transpose(dot_last(values, table))
 
 
 def fourier_call(nb, pc, cap, pair_slot, owner_slot, spectra):
     gc = 8
+    rows = 2 * FIELDS * pc
     return pl.pallas_call(
         functools.partial(fourier_kernel, nb, pc, cap, gc),
-        grid=(2 * FIELDS // gc,),
         in_specs=[
             pl.BlockSpec(memory_space=pltpu.SMEM),
-            pl.BlockSpec(owner_slot.shape, lambda i: (0, 0)),
-            pl.BlockSpec((pc, gc, COEFS), lambda i: (0, i, 0)),
+            pl.BlockSpec(memory_space=pltpu.VMEM),
+            pl.BlockSpec(memory_space=pl.ANY),
         ],
-        out_specs=pl.BlockSpec((nb, gc, LANES), lambda i: (0, i, 0)),
         out_shape=jax.ShapeDtypeStruct((nb, 2 * FIELDS, LANES), f32),
         scratch_shapes=[
-            pltpu.VMEM((2, 4 * nb, 2 * COEF_PAD), bf16),
-            pltpu.VMEM((3, nb, LANES), f32),
-            pltpu.VMEM((HALF, LANES), jnp.int32),
-            pltpu.VMEM((2, gc * HALF, 2 * COEF_PAD), bf16),
+            pltpu.VMEM(spectra.shape, f32),
+            pltpu.VMEM((4 * nb, COEF_PAD), bf16),
+            pltpu.VMEM((pc * gc, LANES), jnp.int32),
+            pltpu.VMEM((2, rows, COEF_PAD), bf16),
+            pltpu.VMEM((2, rows, COEF_PAD - (EARLY + 1) * LANES), bf16),
+            pltpu.SemaphoreType.DMA((2 * FIELDS // gc,)),
         ],
         compiler_params=pltpu.CompilerParams(vmem_limit_bytes=VMEM_LIMIT),
         name="fourier",

time: 77.5 us -> 62.1 us (0.80)
  Pallas kernels: 39.4 us -> 24 us
    pallas_call x1, Pallas kernels: 24.2 us -> 8.77 us  [fourier_call(): pl.pallas_call(functools.partial(fourier_kernel, nb, pc, cap, gc), in_spe...]
  transfers between devices with their start and end apart: 1 -> 1, of which waited for: 1 -> 1; matrix products, arithmetic and copies ran while one was open for 4% -> 4% of each run, Pallas kernels for 4% -> 6%
where the time goes in v1:
time: 62.1 us; the launch traced here: 61.7 us
  blocking collectives  25.1 us (40%)
  Pallas kernels  24 us (39%)
  starting transfers between devices  7.29 us (12%)
  local copies, waits for them, and re-layouts  3.41 us (5%)
  waiting for transfers between devices  1.18 us (2%)
  between operations  0.67 us (1%)
    all_to_all x1, blocking collectives, body(): lax.all_to_all(outbound, 'fld', split_axis=0, concat_axis=0, tiled=True)  13.1 us
    all_to_all x1, blocking collectives, body(): lax.all_to_all(copies, ('band', 'fld'), split_axis=0, concat_axis=0, tile...  12.1 us
    pallas_call x1, Pallas kernels, advance_call(): pl.pallas_call(functools.partial(advance_kernel, nb, cp, ndev, lc), in_sp...  9.79 us
    pallas_call x1, Pallas kernels, fourier_call(): pl.pallas_call(functools.partial(fourier_kernel, nb, pc, cap, gc), in_spe...  8.77 us
    all_to_all x1, starting transfers between devices, body(): lax.all_to_all(coeffs, 'fld', split_axis=0, concat_axis=0, tiled=True)  7.29 us
    pallas_call x1, Pallas kernels, prepare_call(): pl.pallas_call(functools.partial(prepare_kernel, nb, pc, cp), out_shape=[...  3.4 us
    pallas_call x1, Pallas kernels, owned_call(): pl.pallas_call(functools.partial(owned_kernel, nb, cap, cp, scale), out_s...  2.02 us
    unnamed x7, local copies, waits for them, and re-layouts  1.42 us
  transfers between devices with their start and end apart: 1, of which 1 were waited for; matrix products, arithmetic and copies ran while one was open for 4% of the time, Pallas kernels for 6%

profile of v1, /device:TPU:0, one launch (start us, length us, event | category | flops | bytes accessed | tf_op | source)
XLA Modules:
  0.0 61.7 jit_solution(1539288417706444673)
XLA Ops:
  0.6 0.0 copy-start.2
  0.6 0.0 copy-start.1
  0.7 8.8 %fourier.1 = f32[8,32,128]{2,1,0:T(8,128)} custom-call(s32[480]{0:T(512)} %pairs_ref.1, s32[1,640]{1,0:T(1,128)} %slot_ref.3, f32[60,32,961]{2,1,0:T(8,128)} %spec_ref.1), custom_call_target="tpu_custom_call" | custom-call | tf_op jit(solution)/shard_map/fourier/pallas_call | solution.py:179
  9.4 7.3 %all-to-all-start = ((f32[8,32,128]{2,1,0:T(8,128)}), f32[8,32,128]{2,1,0:T(8,128)S(1)}, u32[]{:S(2)}, u32[]{:S(2)}) async-start(f32[8,32,128]{2,1,0:T(8,128)} %fourier.1), calls=%async_computation | async-start | bytes 262144 | tf_op jit(solution)/shard_map/all_to_all | solution.py:490
  16.7 0.0 copy-done.1
  16.7 0.8 %copy.14.win_ref = f32[256,33]{1,0:T(8,128)} copy(f32[256,33]{0,1:T(8,128)S(1)} %copy-done.1) | data formatting | bytes 67584 | tf_op args[8]
  17.5 1.2 %slice.3.owner_ref = s32[1,128]{1,0:T(1,128)} slice(s32[1,1920]{1,0:T(1,128)} %param.13), slice={[0:1], [0:128]} | slice | bytes 1024 | tf_op jit(solution)/shard_map/slice | solution.py:437
  18.7 0.0 copy-done.2
  18.7 0.8 %broadcast_in_dim.4.pairs_ref = s32[480,128]{1,0:T(8,128)} broadcast(s32[480]{0:T(512)S(1)} %copy-done.2), dimensions={0} | broadcast | bytes 247680 | tf_op jit(solution)/shard_map/broadcast_in_dim | solution.py:492
  19.5 3.4 %prepare.1 = (f32[32,2048]{1,0:T(8,128)}, f32[8,2048]{1,0:T(8,128)}, s32[8,1024]{1,0:T(8,128)}, bf16[384,256]{1,0:T(8,128)(2,1)}, f32[32,128]{1,0:T(8,128)}, /*i...) custom-call(s32[480,128]{1,0:T(8,128)} %broadcast_in_dim.4.pairs_ref, ...), custom_call_target="tpu_custom_call" | custom-call | tf_op jit(solution)/shard_map/prepare/pallas_call | solution.py:303
  22.9 1.2 %all-to-all-done.arrived_ref = f32[8,32,128]{2,1,0:T(8,128)S(1)} async-done(((f32[8,32,128]{2,1,0:T(8,128)}), f32[8,32,128]{2,1,0:T(8,128)S(1)}, u32[]{:S(2)}, u32[]{:S(2)}) %all-to-all-start) | async-done | bytes 131104 | tf_op jit(solution)/shard_map/all_to_all | solution.py:490
  24.1 0.0 copy-start
  24.1 0.6 %copy-done = f32[8,32,128]{2,1,0:T(8,128)} copy-done((f32[8,32,128]{2,1,0:T(8,128)}, f32[8,32,128]{2,1,0:T(8,128)S(1)}, u32[]{:S(2)}) %copy-start) | copy-done | bytes 131096
  24.7 9.8 %advance.1 = (f32[8,32,256]{2,1,0:T(8,128)}, f32[32,16]{1,0:T(8,128)}) custom-call(s32[1,128]{1,0:T(1,128)} %slice.3.owner_ref, f32[8,32,128]{2,1,0:T(8,128)} %copy-done, s32[8,1024]{1,0:T(8,128)} %get-tuple-element.18.inverse_ref, bf16[384,256]{1,0:T(8,128)(2,1)} %get-tuple-element.19.dft_ref, f32[32,128]{1,0:T(8,128)} %get-tuple-element.20.turn_ref, ...), custom_call_target="tpu_custom_call" | custom-call | tf_op jit(solution)/shard_map/advance/pallas_call | solution.py:418
  34.5 12.1 %all_to_all.21 = f32[32,1,16]{2,1,0:T(1,128)} all-to-all(f32[32,1,16]{2,1,0:T(1,128)} %bitcast.7), channel_id=1, replica_groups=mesh['band'=4,'fld'=8] {'band','fld'}, dimensions={0} | all-to-all | bytes 4096 | tf_op jit(solution)/shard_map/all_to_all | solution.py:497
  46.6 13.1 %all_to_all.22.received_ref = f32[8,32,256]{2,1,0:T(8,128)} all-to-all(f32[8,32,256]{2,1,0:T(8,128)} %get-tuple-element.28), channel_id=1, replica_groups=mesh['band'=4,'fld'=8] {'fld'}, dimensions={0} | all-to-all | bytes 524288 | tf_op jit(solution)/shard_map/all_to_all | solution.py:496
  59.6 2.0 %owned.1 = (f32[16,640]{1,0:T(8,128)}, f32[16,640]{1,0:T(8,128)}, f32[1,16]{1,0:T(1,128)}) custom-call(s32[1,640]{1,0:T(1,128)} %slot_ref.3, f32[8,32,256]{2,1,0:T(8,128)} %all_to_all.22.received_ref, f32[32,16]{1,0:T(8,128)} %bitcast.6), custom_call_target="tpu_custom_call" | custom-call | tf_op jit(solution)/shard_map/owned/pallas_call | solution.py:460
Async XLA Ops:
  0.6 18.0 %copy-start.2 = (s32[480]{0:T(512)S(1)}, s32[480]{0:T(512)}, u32[]{:S(2)}) copy-start(s32[480]{0:T(512)} %pairs_ref.1) | copy-start | bytes 5764
  0.6 16.1 %copy-start.1 = (f32[256,33]{0,1:T(8,128)S(1)}, f32[256,33]{0,1:T(8,128)}, u32[]{:S(2)}) copy-start(f32[256,33]{0,1:T(8,128)} %param.18) | copy-start | bytes 101380
  9.4 14.6 %all-to-all-start = ((f32[8,32,128]{2,1,0:T(8,128)}), f32[8,32,128]{2,1,0:T(8,128)S(1)}, u32[]{:S(2)}, u32[]{:S(2)}) async-start(f32[8,32,128]{2,1,0:T(8,128)} %fourier.1), calls=%async_computation | async-start | bytes 262144 | tf_op jit(solution)/shard_map/all_to_all | solution.py:490
  24.1 0.6 %copy-start = (f32[8,32,128]{2,1,0:T(8,128)}, f32[8,32,128]{2,1,0:T(8,128)S(1)}, u32[]{:S(2)}) copy-start(f32[8,32,128]{2,1,0:T(8,128)S(1)} %all-to-all-done.arrived_ref) | copy-start | bytes 393220

commit v2 on v1

--- a/solution.py
+++ b/solution.py
@@ -99,19 +99,26 @@
         at = pl.ds(t * LANES, LANES)
         tab[0 : 2 * nb, at] = high
         tab[2 * nb : 4 * nb, at] = low
-    row = jnp.zeros((nb, LANES), f32)
-    for s in range(pc):
-        pair = pairs_ref[first + s]
-        row = jnp.where(lane % HALF == s, pair.astype(f32), row)
-        thr[s * gc : (s + 1) * gc, :] = jnp.full((gc, LANES), WAVES - pair, jnp.int32)
-    sine, cosine = sincos_turns(row * odd)
-    is_odd = row - 2.0 * jnp.floor(row * 0.5) == 1.0
-    alpha = jnp.where(is_odd, sine, cosine)
-    beta = jnp.where(is_odd, cosine, -sine)
-    sine, cosine = sincos_turns(odd)
-    gamma = jnp.where(is_odd, cosine, -sine)
-    delta = jnp.where(is_odd, sine, cosine)
     pieces = -(-rows // LANES)
+    per_piece = LANES // gc
+    sine1, cosine1 = sincos_turns(odd)
+    factors = []
+    for i in range(pieces):
+        row = jnp.zeros((nb, LANES), f32)
+        for s in range(i * per_piece, min((i + 1) * per_piece, pc)):
+            pair = pairs_ref[first + s]
+            row = jnp.where(lane // gc == s - i * per_piece, pair.astype(f32), row)
+            thr[s * gc : (s + 1) * gc, :] = jnp.full((gc, LANES), WAVES - pair, jnp.int32)
+        sine, cosine = sincos_turns(row * odd)
+        is_odd = row - 2.0 * jnp.floor(row * 0.5) == 1.0
+        factors.append(
+            (
+                jnp.where(is_odd, sine, cosine),
+                jnp.where(is_odd, cosine, -sine),
+                jnp.where(is_odd, cosine1, -sine1),
+                jnp.where(is_odd, sine1, cosine1),
+            )
+        )
     wide = iota((rows, LANES), 1)
     for k in range(groups):
         copies[k].wait()
@@ -149,16 +156,15 @@
         shifted = shifted[: 2 * nb] + shifted[2 * nb :]
         pad = [(0, 0), (0, pieces * LANES - rows)]
         first_part, shifted = jnp.pad(everything - shifted, pad), jnp.pad(shifted, pad)
+        waves = []
+        for i, (alpha, beta, gamma, delta) in enumerate(factors):
+            at = slice(i * LANES, (i + 1) * LANES)
+            waves.append(alpha * first_part[:nb, at] + beta * first_part[nb:, at])
+            waves.append(gamma * shifted[:nb, at] + delta * shifted[nb:, at])
         for g in range(gc):
             source = (iota((1, LANES), 1) % HALF) * gc + g
-            piece_at, lane_at = source // LANES, source % LANES
-
-            def gather(values):
-                return pick((pieces, lambda i: values[:, i * LANES : (i + 1) * LANES]), piece_at, lane_at, nb)
-
-            wave0 = alpha * gather(first_part[:nb]) + beta * gather(first_part[nb:])
-            wave1 = gamma * gather(shifted[:nb]) + delta * gather(shifted[nb:])
-            value = jnp.where(lane < HALF, wave0, wave1)
+            piece_at = 2 * (source // LANES) + iota((1, LANES), 1) // HALF
+            value = pick((2 * pieces, lambda i: waves[i]), piece_at, source % LANES, nb)
             value = jnp.where(lane % HALF < pc, value, 0.0)
             if k == 0 and g == 0:
                 slot = jnp.broadcast_to(slot_ref[...], (nb, slot_ref.shape[1]))
@@ -197,7 +203,7 @@
     )(pair_slot, owner_slot, spectra)
 
 
-def prepare_kernel(nb, pc, cp, pairs_ref, land_ref, state_ref, target_ref, amp_ref, win_ref, wout_ref,
+def prepare_kernel(nb, pc, cp, pairs_ref, owner_ref, land_ref, state_ref, target_ref, amp_ref, win_ref, wout_ref,
                    cells_ref, place_ref, inverse_ref, dft_ref, turn_ref, amps_ref,
                    wx_ref, wo_ref, wt_ref, wb_ref):
     lane = iota((1, LANES), 1)
@@ -229,21 +235,16 @@
             hour = iota((8, LANES), 0).astype(f32)
             turns = column.astype(f32) * (1.0 / LONS) + hour * (1.0 / 24.0)
             forcing = jnp.maximum(sincos_turns(turns)[1], 0.0) * sin_colat
-            place_ref[:, at] = jnp.where(iota((8, LANES), 0) < STEPS, forcing, column.astype(f32))
-    for q in range(WAVE_INNER // 2):
-        natural = lane + q * LANES
-        wave = (natural % HALF) * WAVE_INNER + natural // HALF
-        pair = jnp.minimum(wave, WAVES - 1 - wave)
-        total = jnp.zeros((8, LANES), jnp.int32)
-        rows = iota((8, LANES), 0)
-        for i in range(PAIRS // 8):
-            here = i * 8 + rows
-            arrives = here + ((here.astype(f32) + 0.5) * (1.0 / pc)).astype(jnp.int32) * (LANES - pc)
-            total = total + jnp.where(pairs_ref[i * 8 : i * 8 + 8, :] == pair, arrives, 0)
-        found = jnp.sum(total.astype(f32), axis=0, keepdims=True).astype(jnp.int32)
-        inverse_ref[:, pl.ds(q * LANES, LANES)] = jnp.broadcast_to(
-            found + jnp.where(wave >= PAIRS, HALF, 0), (8, LANES)
-        )
+            rest = jnp.where(iota((8, LANES), 0) == STEPS, column, owner_ref[0:1, 0:1]).astype(f32)
+            place_ref[:, at] = jnp.where(iota((8, LANES), 0) < STEPS, forcing, rest)
+    natural = iota((8, LANES), 0) * LANES + iota((8, LANES), 1)
+    wave = (natural % HALF) * WAVE_INNER + natural // HALF
+    pair = jnp.minimum(wave, WAVES - 1 - wave)
+    totals = [jnp.where(wave >= PAIRS, HALF, 0)] + [jnp.zeros((8, LANES), jnp.int32)] * 3
+    for i in range(PAIRS):
+        arrives = i // pc * LANES + i % pc
+        totals[i % 4] = jnp.where(pair == pairs_ref[i], totals[i % 4] + arrives, totals[i % 4])
+    inverse_ref[...] = totals[0] + totals[1] + totals[2] + totals[3]
     a = iota((HALF, LANES), 0)
     sine, cosine = sincos_turns((a * iota((HALF, LANES), 1)).astype(f32) * (1.0 / LANES))
     table = jnp.concatenate(
@@ -262,9 +263,12 @@
     amps_ref[...] = jnp.broadcast_to(
         jnp.sum(jnp.where(diagonal, amp, 0.0), axis=1, keepdims=True), (FIELDS, LANES)
     )
-    win = win_ref[...]
+    turned = win_ref[...]
     wout = wout_ref[...]
-    high, low = halves(win)
+    high, low = halves(turned[:joined])
+    wt_ref[0:joined, :] = high
+    wt_ref[joined : 2 * joined, :] = low
+    high, low = halves(jnp.transpose(turned))
     s, p = slice(0, STATE), slice(STATE, joined)
     tail = jnp.where(iota((UNITS, STATE), 1) == 0, high[:, joined:].astype(f32), 0.0)
     tail = jnp.where(iota((UNITS, STATE), 1) == 1, low[:, joined:].astype(f32), tail)
@@ -273,10 +277,6 @@
     wx_ref[...] = jnp.concatenate(
         [hf[:, s], lf[:, s], hf[:, s], hf[:, p], lf[:, p], hf[:, p], tail], axis=1
     ).astype(bf16)
-    turned = jnp.transpose(win)[:joined]
-    high, low = halves(turned)
-    wt_ref[0:joined, :] = high
-    wt_ref[joined : 2 * joined, :] = low
     high, low = halves(wout)
     wo_ref[0:STATE, :] = high
     wo_ref[STATE : 2 * STATE, :] = low
@@ -291,7 +291,7 @@
     shapes = [
         ((2 * STATE, length), f32),
         ((8, length), f32),
-        ((8, WAVE_INNER * HALF), jnp.int32),
+        ((8, LANES), jnp.int32),
         ((3 * LANES, 2 * LANES), bf16),
         ((2 * WAVE_INNER, LANES), f32),
         ((FIELDS, LANES), f32),
@@ -300,16 +300,18 @@
         ((4 * STATE, UNITS), bf16),
         ((UNITS, 3 * STATE), bf16),
     ]
+    vmem = pl.BlockSpec(memory_space=pltpu.VMEM)
     return pl.pallas_call(
         functools.partial(prepare_kernel, nb, pc, cp),
+        in_specs=[pl.BlockSpec(memory_space=pltpu.SMEM)] + [vmem] * (len(arrays) - 1),
         out_shape=[jax.ShapeDtypeStruct(*s) for s in shapes],
         compiler_params=pltpu.CompilerParams(vmem_limit_bytes=VMEM_LIMIT),
         name="prepare",
     )(*arrays)
 
 
-def advance_kernel(nb, cp, ndev, lc, owner_ref, arrived_ref, inverse_ref, dft_ref, turn_ref, amps_ref, cells_ref,
-                   place_ref, wx_ref, wo_ref, wt_ref, wb_ref, out_ref, copies_ref,
+def advance_kernel(nb, cap, cp, lc, arrived_ref, inverse_ref, dft_ref, turn_ref, amps_ref, cells_ref,
+                   place_ref, wx_ref, wo_ref, wt_ref, wb_ref, out_ref,
                    grid_ref, pattern_ref, param_ref, force_ref, state_ref, slope_ref, adj_ref, grad_ref):
     length = nb * cp
     lane = iota((1, LANES), 1)
@@ -319,7 +321,7 @@
     for q in range(WAVE_INNER // 2):
         natural = lane + q * LANES
         wave = (natural % HALF) * WAVE_INNER + natural // HALF
-        at = inverse_ref[0:1, pl.ds(q * LANES, LANES)]
+        at = inverse_ref[q : q + 1, :]
         x = pick((nb, lambda i: arrived_ref[i]), at // LANES, at % LANES, 2 * FIELDS)
         x = jnp.where(wave < WAVES, x * jnp.where(wave == 0, 1.0, 2.0), 0.0)
         real, imag = x[:FIELDS], x[FIELDS:]
@@ -393,35 +395,32 @@
             adj_ref[:, at] = adjoint + both[:STATE]
             gained = both[STATE:]
             grad_ref[:, at] = gained if t == STEPS - 1 else grad_ref[:, at] + gained
-    first_owner = owner_ref[0, 0]
+    first_owner = jnp.max(place_ref[STEPS + 1 : STEPS + 2, 0:LANES]).astype(jnp.int32)
     total = jnp.zeros((FIELDS, cp), f32)
-    place = iota((FIELDS, cp), 1).astype(f32)
+    place = iota((FIELDS, cp), 1)
     for m in range(nb):
-        owner = (first_owner + m) % nb
+        owner = lax.rem(first_owner + m, nb)
         at = pl.ds(m * cp, cp)
-        grad = grad_ref[:, at]
-        out_ref[owner, 0:STATE, :] = state_ref[:, at]
-        out_ref[owner, STATE : 2 * STATE, :] = grad
         count = arrived_ref[owner, 0:1, COUNT_LANE : COUNT_LANE + 1]
-        total = total + jnp.where(place < count, grad * pattern_ref[:, at], 0.0)
+        product = grad_ref[:, at] * pattern_ref[:, at]
+        total = total + jnp.where(place.astype(f32) < count, product, 0.0)
     summed = jnp.sum(total, axis=1, keepdims=True)
-    diagonal = iota((FIELDS, FIELDS), 0) == iota((FIELDS, FIELDS), 1)
-    along = jnp.sum(jnp.where(diagonal, summed, 0.0), axis=0, keepdims=True)
-    copies_ref[...] = jnp.broadcast_to(along, (ndev, FIELDS))
-
-
-def advance_call(nb, cp, ndev, owner_map, arrived, prepared):
+    for m in range(nb):
+        owner = lax.rem(first_owner + m, nb)
+        at = pl.ds(m * cp, cp)
+        out_ref[owner, 0:STATE, :] = jnp.where(place == cap, summed, state_ref[:, at])
+        out_ref[owner, STATE : 2 * STATE, :] = grad_ref[:, at]
+
+
+def advance_call(nb, cap, cp, arrived, prepared):
     cells, place, inverse, dft, turn, amps, wx, wo, wt, wb = prepared
     length = nb * cp
     lc = 512
     vmem = pl.BlockSpec(memory_space=pltpu.VMEM)
     return pl.pallas_call(
-        functools.partial(advance_kernel, nb, cp, ndev, lc),
-        in_specs=[pl.BlockSpec(memory_space=pltpu.SMEM)] + [vmem] * 11,
-        out_shape=[
-            jax.ShapeDtypeStruct((nb, 2 * STATE, cp), f32),
-            jax.ShapeDtypeStruct((ndev, FIELDS), f32),
-        ],
+        functools.partial(advance_kernel, nb, cap, cp, lc),
+        in_specs=[vmem] * 11,
+        out_shape=jax.ShapeDtypeStruct((nb, 2 * STATE, cp), f32),
         scratch_shapes=[
             pltpu.VMEM((LON_OUTER, FIELDS, LANES), f32),
             pltpu.VMEM((FIELDS, length), f32),
@@ -434,10 +433,10 @@
         ],
         compiler_params=pltpu.CompilerParams(vmem_limit_bytes=VMEM_LIMIT),
         name="advance",
-    )(owner_map[:, :LANES], arrived, inverse, dft, turn, amps, cells, place, wx, wo, wt, wb)
-
-
-def owned_kernel(nb, cap, cp, scale, slot_ref, received_ref, parts_ref, final_ref, grad_ref, amp_ref):
+    )(arrived, inverse, dft, turn, amps, cells, place, wx, wo, wt, wb)
+
+
+def owned_kernel(nb, cap, cp, slot_ref, received_ref, final_ref, grad_ref):
     per_row = cp // LANES
     for q in range(slot_ref.shape[1] // LANES):
         at = pl.ds(q * LANES, LANES)
@@ -452,21 +451,19 @@
         found = pick((nb * per_row, load), piece, place % LANES, 2 * STATE)
         final_ref[:, at] = found[:STATE]
         grad_ref[:, at] = found[STATE:]
-    amp_ref[...] = jnp.sum(parts_ref[...], axis=0, keepdims=True) * scale
-
-
-def owned_call(nb, cap, cp, scale, owner_slot, received, parts):
+
+
+def owned_call(nb, cap, cp, owner_slot, received):
     mean = owner_slot.shape[1]
     return pl.pallas_call(
-        functools.partial(owned_kernel, nb, cap, cp, scale),
+        functools.partial(owned_kernel, nb, cap, cp),
         out_shape=[
             jax.ShapeDtypeStruct((STATE, mean), f32),
             jax.ShapeDtypeStruct((FIELDS, mean), f32),
-            jax.ShapeDtypeStruct((1, FIELDS), f32),
         ],
         compiler_params=pltpu.CompilerParams(vmem_limit_bytes=VMEM_LIMIT),
         name="owned",
-    )(owner_slot, received, parts)
+    )(owner_slot, received)
 
 
 def body(
@@ -489,15 +486,19 @@
     coeffs = fourier_call(nb, pc, cap, pair_slot, owner_slot, spectra)
     arrived = lax.all_to_all(coeffs, "fld", split_axis=0, concat_axis=0, tiled=True)
     prepared = prepare_call(
-        nb, pc, cp, jnp.broadcast_to(pair_slot[:, None], (PAIRS, LANES)), land_column, state_start, targets,
-        amplitudes[None, :], weight_in, weight_out,
+        nb, pc, cp, pair_slot, owner_map, land_column, state_start, targets,
+        amplitudes[None, :], jnp.transpose(weight_in), weight_out,
     )
-    outbound, copies = advance_call(nb, cp, ndev, owner_map, arrived, prepared)
+    outbound = advance_call(nb, cap, cp, arrived, prepared)
     received = lax.all_to_all(outbound, "fld", split_axis=0, concat_axis=0, tiled=True)
-    parts = lax.all_to_all(copies, ("band", "fld"), split_axis=0, concat_axis=0, tiled=True)
-    scale = 1.0 / math.sqrt(ndev * ROW_MEAN)
-    final_state, param_grad, amplitude_grad = owned_call(nb, cap, cp, scale, owner_slot, received, parts)
-    return (final_state, param_grad, amplitude_grad[0])
+    total = jnp.sum(received[:, :FIELDS, cap], axis=0)
+    bands = lax.axis_size("band")
+    step = 1
+    while step < bands:
+        total = total + lax.ppermute(total, "band", [(i, i ^ step) for i in range(bands)])
+        step *= 2
+    final_state, param_grad = owned_call(nb, cap, cp, owner_slot, received)
+    return (final_state, param_grad, total / math.sqrt(ndev * ROW_MEAN))
 
 
 def solution(mesh):

time: 62.1 us -> 51.3 us (0.83)
  blocking collectives: 25.1 us -> 11.5 us
  waiting for transfers between devices: 1.18 us -> 5.01 us
  local copies, waits for them, and re-layouts: 3.41 us -> 0.65 us
  starting transfers between devices: 7.29 us -> 8.85 us
  other arithmetic: 0 us -> 0.71 us
    all_to_all x1 -> x0, blocking collectives: 12.1 us -> none  [body(): lax.all_to_all(copies, ('band', 'fld'), split_axis=0, concat_axis=0, tile...]
    all_to_all x1, waiting for transfers between devices: 1.18 us -> 3.89 us  [body(): lax.all_to_all(coeffs, 'fld', split_axis=0, concat_axis=0, tiled=True)]
    ppermute x0 -> x2, starting transfers between devices: none -> 1.56 us  [body(): lax.ppermute(total, 'band', [(i, i ^ step) for i in range(bands)])]
    all_to_all x1, blocking collectives: 13.1 us -> 11.5 us  [body(): lax.all_to_all(outbound, 'fld', split_axis=0, concat_axis=0, tiled=True)]
    slice x1 -> x0, local copies, waits for them, and re-layouts: 1.17 us -> none  [advance_call(): owner_map[:, :LANES]]
    ppermute x0 -> x2, waiting for transfers between devices: none -> 1.12 us  [body(): lax.ppermute(total, 'band', [(i, i ^ step) for i in range(bands)])]
    broadcast_in_dim x1 -> x0, local copies, waits for them, and re-layouts: 0.82 us -> none  [body(): jnp.broadcast_to(pair_slot[:, None], (PAIRS, LANES))]
    unnamed x7 -> x4, local copies, waits for them, and re-layouts: 1.42 us -> 0.65 us
  transfers between devices with their start and end apart: 1 -> 3, of which waited for: 1 -> 2; matrix products, arithmetic and copies ran while one was open for 4% -> 0% of each run, Pallas kernels for 6% -> 11%
where the time goes in v2:
time: 51.3 us; the launch traced here: 50.9 us
  Pallas kernels  23.5 us (46%)
  blocking collectives  11.5 us (22%)
  starting transfers between devices  8.85 us (17%)
  waiting for transfers between devices  5.01 us (10%)
  other arithmetic  0.71 us (1%)
  between operations  0.66 us (1%)
  local copies, waits for them, and re-layouts  0.65 us (1%)
    all_to_all x1, blocking collectives, body(): lax.all_to_all(outbound, 'fld', split_axis=0, concat_axis=0, tiled=True)  11.5 us
    pallas_call x1, Pallas kernels, advance_call(): pl.pallas_call(functools.partial(advance_kernel, nb, cap, cp, lc), in_spe...  9.89 us
    pallas_call x1, Pallas kernels, fourier_call(): pl.pallas_call(functools.partial(fourier_kernel, nb, pc, cap, gc), in_spe...  8.09 us
    all_to_all x1, starting transfers between devices, body(): lax.all_to_all(coeffs, 'fld', split_axis=0, concat_axis=0, tiled=True)  7.29 us
    all_to_all x1, waiting for transfers between devices, body(): lax.all_to_all(coeffs, 'fld', split_axis=0, concat_axis=0, tiled=True)  3.89 us
    pallas_call x1, Pallas kernels, prepare_call(): pl.pallas_call(functools.partial(prepare_kernel, nb, pc, cp), in_specs=[p...  3.45 us
    pallas_call x1, Pallas kernels, owned_call(): pl.pallas_call(functools.partial(owned_kernel, nb, cap, cp), out_shape=[j...  2.03 us
    ppermute x2, starting transfers between devices, body(): lax.ppermute(total, 'band', [(i, i ^ step) for i in range(bands)])  1.56 us
  transfers between devices with their start and end apart: 3, of which 2 were waited for; matrix products, arithmetic and copies ran while one was open for 0% of the time, Pallas kernels for 11%

profile of v2, /device:TPU:0, one launch (start us, length us, event | category | flops | bytes accessed | tf_op | source)
XLA Modules:
  0.0 50.9 jit_solution(8872725267230582577)
XLA Ops:
  0.6 8.1 %fourier.1 = f32[8,32,128]{2,1,0:T(8,128)} custom-call(s32[480]{0:T(512)} %pairs_ref.3, s32[1,640]{1,0:T(1,128)} %slot_ref.3, f32[60,32,961]{2,1,0:T(8,128)} %spec_ref.1), custom_call_target="tpu_custom_call" | custom-call | tf_op jit(solution)/shard_map/fourier/pallas_call | solution.py:185
  8.7 7.3 %all-to-all-start = ((f32[8,32,128]{2,1,0:T(8,128)}), f32[8,32,128]{2,1,0:T(8,128)S(1)}, u32[]{:S(2)}, u32[]{:S(2)}) async-start(f32[8,32,128]{2,1,0:T(8,128)} %fourier.1), calls=%async_computation | async-start | bytes 262144 | tf_op jit(solution)/shard_map/all_to_all | solution.py:487
  16.0 3.5 %prepare.1 = (f32[32,2048]{1,0:T(8,128)}, f32[8,2048]{1,0:T(8,128)}, s32[8,128]{1,0:T(8,128)}, bf16[384,256]{1,0:T(8,128)(2,1)}, f32[32,128]{1,0:T(8,128)}, /*in...) custom-call(s32[480]{0:T(512)} %pairs_ref.3, ...), custom_call_target="tpu_custom_call" | custom-call | tf_op jit(solution)/shard_map/prepare/pallas_call | solution.py:304
  19.5 3.9 %all-to-all-done.arrived_ref = f32[8,32,128]{2,1,0:T(8,128)S(1)} async-done(((f32[8,32,128]{2,1,0:T(8,128)}), f32[8,32,128]{2,1,0:T(8,128)S(1)}, u32[]{:S(2)}, u32[]{:S(2)}) %all-to-all-start) | async-done | bytes 131104 | tf_op jit(solution)/shard_map/all_to_all | solution.py:487
  23.4 0.0 copy-start.1
  23.4 0.6 %copy-done.1 = f32[8,32,128]{2,1,0:T(8,128)} copy-done((f32[8,32,128]{2,1,0:T(8,128)}, f32[8,32,128]{2,1,0:T(8,128)S(1)}, u32[]{:S(2)}) %copy-start.1) | copy-done | bytes 131096
  24.0 9.9 %advance.1 = f32[8,32,256]{2,1,0:T(8,128)} custom-call(f32[8,32,128]{2,1,0:T(8,128)} %copy-done.1, s32[8,128]{1,0:T(8,128)} %get-tuple-element.15.inverse_ref, bf16[384,256]{1,0:T(8,128)(2,1)} %get-tuple-element.16.dft_ref, f32[32,128]{1,0:T(8,128)} %get-tuple-element.17.turn_ref, f32[16,128]{1,0:T(8,128)} %get-tuple-element.18.amps_ref, ...), custom_call_target="tpu_custom_call" | custom-call | tf_op jit(solution)/shard_map/advance/pallas_call | solution.py:420
  33.9 11.5 %all_to_all.10.received_ref = f32[8,32,256]{2,1,0:T(8,128)S(1)} all-to-all(f32[8,32,256]{2,1,0:T(8,128)} %advance.1), channel_id=1, replica_groups=mesh['band'=4,'fld'=8] {'fld'}, dimensions={0} | all-to-all | bytes 524288 | tf_op jit(solution)/shard_map/all_to_all | solution.py:493
  45.4 0.0 copy-start
  45.4 0.2 slice_reduce_fusion
  45.6 0.1 collective-permute-start
  45.7 1.1 %collective-permute-done = f32[16]{0:T(128)S(1)} collective-permute-done((f32[16]{0:T(128)S(1)}, f32[16]{0:T(128)S(1)}, u32[]{:S(2)}, u32[]{:S(2)}) %collective-permute-start) | collective-permute-done | bytes 96 | tf_op jit(solution)/shard_map/ppermute | solution.py:498
  46.8 1.5 %collective-permute-start.1 = (f32[16]{0:T(128)S(1)}, f32[16]{0:T(128)S(1)}, u32[]{:S(2)}, u32[]{:S(2)}) collective-permute-start(f32[16]{0:T(128)S(1)} %add.6), channel_id=1, source_target_pairs={{0,16},{8,24},{16,0},{24,8},{1,17},{9,25},{17,1},{25,9},{2,18},{10... | collective-permute-start | bytes 200 | tf_op jit(solution)/shard_map/ppermute | solution.py:498
  48.3 0.0 copy-done
  48.3 2.0 %owned.1 = (f32[16,640]{1,0:T(8,128)}, f32[16,640]{1,0:T(8,128)}) custom-call(s32[1,640]{1,0:T(1,128)} %slot_ref.3, f32[8,32,256]{2,1,0:T(8,128)} %copy-done), custom_call_target="tpu_custom_call" | custom-call | tf_op jit(solution)/shard_map/owned/pallas_call | solution.py:458
  50.4 0.0 collective-permute-done.1
  50.4 0.5 %add_multiply_fusion = f32[16]{0:T(128)} fusion(f32[16]{0:T(128)S(1)} %add.6, f32[16]{0:T(128)S(1)} %collective-permute-done.1), kind=kLoop, calls=%fused_computation.1 | loop fusion | flops 32 | bytes 192 | tf_op jit(solution)/shard_map/div | solution.py:501
  (1 shorter events, 0.0 us)
Async XLA Ops:
  8.7 14.6 %all-to-all-start = ((f32[8,32,128]{2,1,0:T(8,128)}), f32[8,32,128]{2,1,0:T(8,128)S(1)}, u32[]{:S(2)}, u32[]{:S(2)}) async-start(f32[8,32,128]{2,1,0:T(8,128)} %fourier.1), calls=%async_computation | async-start | bytes 262144 | tf_op jit(solution)/shard_map/all_to_all | solution.py:487
  23.4 0.7 %copy-start.1 = (f32[8,32,128]{2,1,0:T(8,128)}, f32[8,32,128]{2,1,0:T(8,128)S(1)}, u32[]{:S(2)}) copy-start(f32[8,32,128]{2,1,0:T(8,128)S(1)} %all-to-all-done.arrived_ref) | copy-start | bytes 393220
  45.4 2.9 %copy-start = (f32[8,32,256]{2,1,0:T(8,128)}, f32[8,32,256]{2,1,0:T(8,128)S(1)}, u32[]{:S(2)}) copy-start(f32[8,32,256]{2,1,0:T(8,128)S(1)} %all_to_all.10.received_ref) | copy-start | bytes 786436
  45.6 1.2 %collective-permute-start = (f32[16]{0:T(128)S(1)}, f32[16]{0:T(128)S(1)}, u32[]{:S(2)}, u32[]{:S(2)}) collective-permute-start(f32[16]{0:T(128)S(1)} %slice_reduce_fusion), channel_id=1, source_target_pairs={{0,8},{8,0},{16,24},{24,16},{1,9},{9,1},{17,25},{25,17},{2,10},{10... | collective-permute-start | bytes 200 | tf_op jit(solution)/shard_map/ppermute | solution.py:498
  46.8 3.5 %collective-permute-start.1 = (f32[16]{0:T(128)S(1)}, f32[16]{0:T(128)S(1)}, u32[]{:S(2)}, u32[]{:S(2)}) collective-permute-start(f32[16]{0:T(128)S(1)} %add.6), channel_id=1, source_target_pairs={{0,16},{8,24},{16,0},{24,8},{1,17},{9,25},{17,1},{25,9},{2,18},{10... | collective-permute-start | bytes 200 | tf_op jit(solution)/shard_map/ppermute | solution.py:498

commit v3 on v2

--- a/solution.py
+++ b/solution.py
@@ -58,6 +58,10 @@
 def halves(x):
     high = x.astype(bf16)
     return high, (x - high.astype(f32)).astype(bf16)
+
+
+def on_chip(x):
+    return pltpu.with_memory_space_constraint(x, pltpu.VMEM)
 
 
 def dot(a, b):
@@ -304,7 +308,7 @@
     return pl.pallas_call(
         functools.partial(prepare_kernel, nb, pc, cp),
         in_specs=[pl.BlockSpec(memory_space=pltpu.SMEM)] + [vmem] * (len(arrays) - 1),
-        out_shape=[jax.ShapeDtypeStruct(*s) for s in shapes],
+        out_shape=[pltpu.VMEM(*s) for s in shapes],
         compiler_params=pltpu.CompilerParams(vmem_limit_bytes=VMEM_LIMIT),
         name="prepare",
     )(*arrays)
@@ -415,7 +419,7 @@
 def advance_call(nb, cap, cp, arrived, prepared):
     cells, place, inverse, dft, turn, amps, wx, wo, wt, wb = prepared
     length = nb * cp
-    lc = 512
+    lc = 256
     vmem = pl.BlockSpec(memory_space=pltpu.VMEM)
     return pl.pallas_call(
         functools.partial(advance_kernel, nb, cap, cp, lc),
@@ -433,7 +437,7 @@
         ],
         compiler_params=pltpu.CompilerParams(vmem_limit_bytes=VMEM_LIMIT),
         name="advance",
-    )(arrived, inverse, dft, turn, amps, cells, place, wx, wo, wt, wb)
+    )(*(on_chip(x) for x in (arrived, inverse, dft, turn, amps, cells, place, wx, wo, wt, wb)))
 
 
 def owned_kernel(nb, cap, cp, slot_ref, received_ref, final_ref, grad_ref):
@@ -463,7 +467,7 @@
         ],
         compiler_params=pltpu.CompilerParams(vmem_limit_bytes=VMEM_LIMIT),
         name="owned",
-    )(owner_slot, received)
+    )(owner_slot, on_chip(received))
 
 
 def body(

time: 51.3 us -> 48.5 us (0.945)
  Pallas kernels: 23.5 us -> 20.4 us
  waiting for transfers between devices: 5.01 us -> 5.92 us
  local copies, waits for them, and re-layouts: 0.65 us -> 0 us
    pallas_call x1, Pallas kernels: 9.89 us -> 7.74 us  [advance_call(): pl.pallas_call(functools.partial(advance_kernel, nb, cap, cp, lc), in_spe...]
    unnamed x4 -> x0, local copies, waits for them, and re-layouts: 0.65 us -> none
    pallas_call x1, Pallas kernels: 3.45 us -> 2.83 us  [prepare_call(): pl.pallas_call(functools.partial(prepare_kernel, nb, pc, cp), in_specs=[p...]
    all_to_all x1, waiting for transfers between devices: 3.89 us -> 4.51 us  [body(): lax.all_to_all(coeffs, 'fld', split_axis=0, concat_axis=0, tiled=True)]
  transfers between devices with their start and end apart: 3 -> 3, of which waited for: 2 -> 3; matrix products, arithmetic and copies ran while one was open for 0% -> 0% of each run, Pallas kernels for 11% -> 10%
where the time goes in v3:
time: 48.5 us; the launch traced here: 48.1 us
  Pallas kernels  20.4 us (42%)
  blocking collectives  11.5 us (24%)
  starting transfers between devices  8.85 us (18%)
  waiting for transfers between devices  5.92 us (12%)
  other arithmetic  0.71 us (1%)
  between operations  0.66 us (1%)
    all_to_all x1, blocking collectives, body(): lax.all_to_all(outbound, 'fld', split_axis=0, concat_axis=0, tiled=True)  11.5 us
    pallas_call x1, Pallas kernels, fourier_call(): pl.pallas_call(functools.partial(fourier_kernel, nb, pc, cap, gc), in_spe...  8.09 us
    pallas_call x1, Pallas kernels, advance_call(): pl.pallas_call(functools.partial(advance_kernel, nb, cap, cp, lc), in_spe...  7.74 us
    all_to_all x1, starting transfers between devices, body(): lax.all_to_all(coeffs, 'fld', split_axis=0, concat_axis=0, tiled=True)  7.29 us
    all_to_all x1, waiting for transfers between devices, body(): lax.all_to_all(coeffs, 'fld', split_axis=0, concat_axis=0, tiled=True)  4.51 us
    pallas_call x1, Pallas kernels, prepare_call(): pl.pallas_call(functools.partial(prepare_kernel, nb, pc, cp), in_specs=[p...  2.83 us
    pallas_call x1, Pallas kernels, owned_call(): pl.pallas_call(functools.partial(owned_kernel, nb, cap, cp), out_shape=[j...  1.75 us
    ppermute x2, starting transfers between devices, body(): lax.ppermute(total, 'band', [(i, i ^ step) for i in range(bands)])  1.56 us
  transfers between devices with their start and end apart: 3, of which 3 were waited for; matrix products, arithmetic and copies ran while one was open for 0% of the time, Pallas kernels for 10%

profile of v3, /device:TPU:0, one launch (start us, length us, event | category | flops | bytes accessed | tf_op | source)
XLA Modules:
  0.0 48.1 jit_solution(9780312237171371505)
XLA Ops:
  0.6 8.1 %fourier.1 = f32[8,32,128]{2,1,0:T(8,128)} custom-call(s32[480]{0:T(512)} %pairs_ref.3, s32[1,640]{1,0:T(1,128)} %slot_ref.3, f32[60,32,961]{2,1,0:T(8,128)} %spec_ref.1), custom_call_target="tpu_custom_call" | custom-call | tf_op jit(solution)/shard_map/fourier/pallas_call | solution.py:189
  8.7 7.3 %all-to-all-start = ((f32[8,32,128]{2,1,0:T(8,128)}), f32[8,32,128]{2,1,0:T(8,128)S(1)}, u32[]{:S(2)}, u32[]{:S(2)}) async-start(f32[8,32,128]{2,1,0:T(8,128)} %fourier.1), calls=%async_computation | async-start | bytes 262144 | tf_op jit(solution)/shard_map/all_to_all | solution.py:491
  16.0 2.8 %prepare.1 = (f32[32,2048]{1,0:T(8,128)S(1)}, f32[8,2048]{1,0:T(8,128)S(1)}, s32[8,128]{1,0:T(8,128)S(1)}, bf16[384,256]{1,0:T(8,128)(2,1)S(1)}, f32[32,128]{1,0...) custom-call(s32[480]{0:T(512)} %pairs_ref.3, ...), custom_call_target="tpu_custom_call" | custom-call | tf_op jit(solution)/shard_map/prepare/pallas_call | solution.py:308
  18.9 4.5 %all-to-all-done.arrived_ref = f32[8,32,128]{2,1,0:T(8,128)S(1)} async-done(((f32[8,32,128]{2,1,0:T(8,128)}), f32[8,32,128]{2,1,0:T(8,128)S(1)}, u32[]{:S(2)}, u32[]{:S(2)}) %all-to-all-start) | async-done | bytes 131104 | tf_op jit(solution)/shard_map/all_to_all | solution.py:491
  23.4 7.7 %advance.1 = f32[8,32,256]{2,1,0:T(8,128)} custom-call(f32[8,32,128]{2,1,0:T(8,128)S(1)} %all-to-all-done.arrived_ref, s32[8,128]{1,0:T(8,128)S(1)} %get-tuple-element.15.inverse_ref, bf16[384,256]{1,0:T(8,128)(2,1)S(1)} %get-tuple-element.16.dft_ref, f32[32,128]{1,0:T(8,128)S(1)} %get-tuple-element.17.turn_ref, f32[16,128]{1,0:T(8,128)S(1)} %get-tuple-element.18.amps_ref, ...), custom_call_target="tpu_custom_call" | custom-call | tf_op jit(solution)/shard_map/advance/pallas_call | solution.py:424
  31.1 11.5 %all_to_all.10.received_ref = f32[8,32,256]{2,1,0:T(8,128)S(1)} all-to-all(f32[8,32,256]{2,1,0:T(8,128)} %advance.1), channel_id=1, replica_groups=mesh['band'=4,'fld'=8] {'fld'}, dimensions={0} | all-to-all | bytes 524288 | tf_op jit(solution)/shard_map/all_to_all | solution.py:497
  42.6 0.2 slice_reduce_fusion
  42.8 0.1 collective-permute-start
  42.9 1.1 %collective-permute-done = f32[16]{0:T(128)S(1)} collective-permute-done((f32[16]{0:T(128)S(1)}, f32[16]{0:T(128)S(1)}, u32[]{:S(2)}, u32[]{:S(2)}) %collective-permute-start) | collective-permute-done | bytes 96 | tf_op jit(solution)/shard_map/ppermute | solution.py:502
  44.0 1.5 %collective-permute-start.1 = (f32[16]{0:T(128)S(1)}, f32[16]{0:T(128)S(1)}, u32[]{:S(2)}, u32[]{:S(2)}) collective-permute-start(f32[16]{0:T(128)S(1)} %add.6), channel_id=1, source_target_pairs={{0,16},{8,24},{16,0},{24,8},{1,17},{9,25},{17,1},{25,9},{2,18},{10... | collective-permute-start | bytes 200 | tf_op jit(solution)/shard_map/ppermute | solution.py:502
  45.5 1.7 %owned.1 = (f32[16,640]{1,0:T(8,128)}, f32[16,640]{1,0:T(8,128)}) custom-call(s32[1,640]{1,0:T(1,128)} %slot_ref.3, f32[8,32,256]{2,1,0:T(8,128)S(1)} %all_to_all.10.received_ref), custom_call_target="tpu_custom_call" | custom-call | tf_op jit(solution)/shard_map/owned/pallas_call | solution.py:462
  47.3 0.3 collective-permute-done.1
  47.6 0.5 %add_multiply_fusion = f32[16]{0:T(128)} fusion(f32[16]{0:T(128)S(1)} %add.6, f32[16]{0:T(128)S(1)} %collective-permute-done.1), kind=kLoop, calls=%fused_computation.1 | loop fusion | flops 32 | bytes 192 | tf_op jit(solution)/shard_map/div | solution.py:505
  (1 shorter events, 0.0 us)
Async XLA Ops:
  8.7 14.6 %all-to-all-start = ((f32[8,32,128]{2,1,0:T(8,128)}), f32[8,32,128]{2,1,0:T(8,128)S(1)}, u32[]{:S(2)}, u32[]{:S(2)}) async-start(f32[8,32,128]{2,1,0:T(8,128)} %fourier.1), calls=%async_computation | async-start | bytes 262144 | tf_op jit(solution)/shard_map/all_to_all | solution.py:491
  42.8 1.2 %collective-permute-start = (f32[16]{0:T(128)S(1)}, f32[16]{0:T(128)S(1)}, u32[]{:S(2)}, u32[]{:S(2)}) collective-permute-start(f32[16]{0:T(128)S(1)} %slice_reduce_fusion), channel_id=1, source_target_pairs={{0,8},{8,0},{16,24},{24,16},{1,9},{9,1},{17,25},{25,17},{2,10},{10... | collective-permute-start | bytes 200 | tf_op jit(solution)/shard_map/ppermute | solution.py:502
  44.0 3.5 %collective-permute-start.1 = (f32[16]{0:T(128)S(1)}, f32[16]{0:T(128)S(1)}, u32[]{:S(2)}, u32[]{:S(2)}) collective-permute-start(f32[16]{0:T(128)S(1)} %add.6), channel_id=1, source_target_pairs={{0,16},{8,24},{16,0},{24,8},{1,17},{9,25},{17,1},{25,9},{2,18},{10... | collective-permute-start | bytes 200 | tf_op jit(solution)/shard_map/ppermute | solution.py:502
